TPU v7x, 32 devices: a whole 2x2x4 slice. The times are simulated.
32 devices in a mesh: groups: 2 (over y), fsdp: 4 (over z), rep: 4 (over x, core).
Axes of the slice: x: 2, y: 2, z: 4, core: 2. Of those that a mesh axis runs over, the one named last changes fastest.
Arguments:
- images: bfloat16 [8, 16, 256, 320], P(('groups', 'rep'), 'fsdp'), parts along dimension 0, may hold values from -60 to 60
- gains: float32 [2, 320], replicated, may hold values from 0.5 to 1.5
- conv_weight: bfloat16 [2880, 320], P('fsdp'), may hold values from -0.109375 to 0.109375
- cotangent: bfloat16 [8, 8, 128, 320], P(('groups', 'rep'), 'fsdp'), parts along dimension 0, may hold values from -60 to 60
Outputs:
- output_maps: bfloat16 [8, 8, 128, 320], P(('groups', 'rep'), 'fsdp'), parts along dimension 0
- input_grad: bfloat16 [8, 16, 256, 320], P(('groups', 'rep'), 'fsdp'), parts along dimension 0
- weight_grad: float32 [5760, 320], P(('groups', 'fsdp')), parts along dimension 0
- gain_grad: float32 [4, 320], P('groups'), parts along dimension 0
There are 2 independent parts, one for each index of `groups`. A program takes and returns all parts, laid end to end along the dimension named above; an argument that names none is the same for every part. Nothing has to cross between parts.
All inputs are finite; a program needn't handle non-finite values.
Results may differ from a plain program's by a relative error of at most 0.0095.
Values may be sent and summed in bfloat16 or wider, within the bound.
A program may use at most 64 MiB of HBM per device.

v0:
```python
import jax
import jax.numpy as jnp
from jax import lax
from jax.sharding import PartitionSpec as P

GROUPS = 32


def passed_along(shard, axis, by):
    size = lax.axis_size(axis)
    pairs = [(i, i + by) for i in range(size) if 0 <= i + by < size]
    return lax.ppermute(shard, axis, pairs)


def spread_taps(first, middle, last, axis):
    length = first.shape[axis]
    widths_end = [(0, 0)] * first.ndim
    widths_end[axis] = (0, 1)
    widths_start = [(0, 0)] * first.ndim
    widths_start[axis] = (1, 0)
    even = jnp.pad(first, widths_end) + jnp.pad(last, widths_start)
    odd = jnp.pad(middle, widths_end)
    merged = jnp.stack([even, odd], axis=axis + 1)
    shape = list(even.shape)
    shape[axis] = 2 * (length + 1)
    merged = merged.reshape(shape)
    return lax.slice_in_dim(merged, 0, 2 * length + 1, axis=axis)


def shards(images, gains, conv_weight, cotangent):
    batch, rows, width, chans = images.shape
    outs_ch = conv_weight.shape[1]
    n_fsdp = lax.axis_size("fsdp")
    per_group = chans // GROUPS
    x_val = images.astype(jnp.float32)
    grouped = x_val.reshape(batch, rows, width, GROUPS, per_group)
    part_one = jnp.sum(grouped, axis=(1, 2, 4))
    part_two = jnp.sum(grouped * grouped, axis=(1, 2, 4))
    full_weight = lax.all_gather(conv_weight, "fsdp", axis=0, tiled=True)
    sum_one, sum_two = lax.psum((part_one, part_two), "fsdp")
    count = rows * n_fsdp * width * per_group
    mean = sum_one / count
    rstd = 1.0 / jnp.sqrt(sum_two / count - mean * mean + 1e-05)
    normed_g = (grouped - mean[:, None, None, :, None]) * rstd[:, None, None, :, None]
    normed = normed_g.reshape(x_val.shape)
    z_val = gains[0] * normed + gains[1]
    act = (z_val * jax.nn.sigmoid(z_val)).astype(jnp.bfloat16)
    above = passed_along(act[:, rows - 1 : rows], "fsdp", 1)
    padded = jnp.concatenate([above, act], axis=1)
    kernel = full_weight.reshape(3, 3, chans, outs_ch)
    result = lax.conv_general_dilated(
        padded,
        kernel,
        (2, 2),
        ((0, 0), (1, 0)),
        dimension_numbers=("NHWC", "HWIO", "NHWC"),
        preferred_element_type=jnp.float32,
    )
    output_maps = result.astype(jnp.bfloat16)
    patch_grad = jnp.einsum(
        "bijo,ko->bijk", cotangent, full_weight, preferred_element_type=jnp.float32
    )
    half_rows, half_cols = (cotangent.shape[1], cotangent.shape[2])
    taps = patch_grad.reshape(batch, half_rows, half_cols, 3, 3, chans)
    by_row = [
        spread_taps(
            taps[:, :, :, row_tap, 0], taps[:, :, :, row_tap, 1], taps[:, :, :, row_tap, 2], 2
        )
        for row_tap in range(3)
    ]
    grid = spread_taps(by_row[0], by_row[1], by_row[2], 1)[:, :, 1:]
    from_below = passed_along(grid[:, 0:1].astype(jnp.bfloat16), "fsdp", -1).astype(jnp.float32)
    filler = jnp.zeros((batch, rows - 1, width, chans), jnp.float32)
    act_grad = grid[:, 1:] + jnp.concatenate([filler, from_below], axis=1)
    padded_cols = jnp.pad(padded, ((0, 0), (0, 0), (1, 0), (0, 0)))
    blocks = []
    for row_tap in range(3):
        for col_tap in range(3):
            window = padded_cols[:, row_tap : row_tap + rows : 2, col_tap : col_tap + width : 2]
            blocks.append(
                jnp.einsum("bijc,bijo->co", window, cotangent, preferred_element_type=jnp.float32)
            )
    total_pixels = batch * lax.axis_size("rep") * half_rows * n_fsdp * half_cols
    scale = 1.0 / jnp.sqrt(jnp.float32(total_pixels))
    weight_term = jnp.concatenate(blocks, axis=0) * scale
    sig = jax.nn.sigmoid(z_val)
    z_grad = act_grad * sig * (1.0 + z_val * (1.0 - sig))
    u_part = jnp.sum(z_grad * normed, axis=(1, 2))
    v_part = jnp.sum(z_grad, axis=(1, 2))
    u_sum, v_sum = lax.psum((u_part, v_part), "fsdp")
    gain_term = jnp.stack([jnp.sum(u_sum, axis=0), jnp.sum(v_sum, axis=0)]) * scale
    su_val = jnp.sum((gains[0] * u_sum).reshape(batch, GROUPS, per_group), axis=-1)
    sv_val = jnp.sum((gains[0] * v_sum).reshape(batch, GROUPS, per_group), axis=-1)
    scaled = (gains[0] * z_grad).reshape(grouped.shape)
    dx_val = rstd[:, None, None, :, None] * (
        scaled
        - sv_val[:, None, None, :, None] / count
        - normed_g * su_val[:, None, None, :, None] / count
    )
    input_grad = dx_val.reshape(x_val.shape).astype(jnp.bfloat16)
    owned = lax.psum_scatter(weight_term, "fsdp", scatter_dimension=0, tiled=True)
    weight_grad, gain_grad = (
        lax.psum(owned.astype(jnp.bfloat16), "rep").astype(jnp.float32),
        lax.psum(gain_term.astype(jnp.bfloat16), "rep").astype(jnp.float32),
    )
    return (output_maps, input_grad, weight_grad, gain_grad)


def solution(mesh):
    in_specs = (
        P(("groups", "rep"), "fsdp", None, None),
        P(),
        P("fsdp", None),
        P(("groups", "rep"), "fsdp", None, None),
    )
    out_specs = (
        P(("groups", "rep"), "fsdp", None, None),
        P(("groups", "rep"), "fsdp", None, None),
        P(("groups", "fsdp"), None),
        P("groups", None),
    )
    return jax.shard_map(shards, mesh=mesh, in_specs=in_specs, out_specs=out_specs, check_vma=False)
```

profile of v0, /device:TPU:0, one launch (start us, length us, event | category | flops | bytes accessed | tf_op | source)
XLA Modules:
  0.0 300.0 jit_solution(18185248881887564390)
XLA Ops:
  7.2 0.7 all-gather.3.cloned.1.call-update
  8.0 1.4 convert_reduce_fusion
  9.8 13.6 %all-reduce.15 = (f32[1,32]{1,0:T(1,128)S(1)}, f32[1,32]{1,0:T(1,128)S(1)}) all-reduce(f32[1,32]{1,0:T(1,128)S(1)} %bitcast.156, f32[1,32]{1,0:T(1,128)S(1)} %bitcast.157), channel_id=1, replica_groups=mesh['groups'=2,'fsdp'=4,'rep'=4] {'fsdp'}, use_global_device_ids=true, to_apply=%region_5.6 | all-reduce | flops 64 | bytes 512 | tf_op jit(solution)/shard_map/psum | solution.py:40
  23.3 32.5 %all-gather.3.cloned.1.call-done = bf16[4,720,320]{1,2,0:T(8,128)(2,1)} async-done(((bf16[1,720,320]{1,2,0:T(8,128)(2,1)}), bf16[4,720,320]{1,2,0:T(8,128)(2,1)}) %all-gather.3.cloned.1.call-update) | async-done | bytes 1843216 | tf_op jit(solution)/shard_map/all_gather | solution.py:39
  55.9 3.0 %copy.34 = bf16[4,720,320]{2,1,0:T(8,128)(2,1)S(1)} copy(bf16[4,720,320]{1,2,0:T(8,128)(2,1)} %all-gather.3.cloned.1.call-done) | data formatting | bytes 3686400 | tf_op jit(solution)/shard_map/all_gather | solution.py:39
  58.9 0.9 convolution_bitcast_fusion
  59.9 0.5 copy-done.1
  60.3 1.0 slice_bitcast_fusion.8
  61.4 0.2 pad_bitcast_fusion.1
  61.7 0.7 copy.44
  62.4 0.3 slice.129
  62.7 1.4 pad_bitcast_fusion
  64.5 0.7 copy.41
  65.2 0.3 slice.125
  65.5 0.7 copy-done.5
  66.3 0.2 pad_bitcast_fusion.3
  66.6 0.7 copy.38
  67.3 0.3 slice.121
  67.6 0.7 add_bitcast_fusion
  68.3 0.7 copy-done.3
  69.0 0.7 pad_maximum_fusion
  69.7 3.8 %copy.45 = f32[1,3,2,257,320]{3,4,2,1,0:T(8,128)} copy(f32[1,3,2,257,320]{4,1,3,2,0:T(4,128)S(1)} %pad_maximum_fusion) | data formatting | bytes 3947520 | tf_op jit(solution)/shard_map/stack | solution.py:23
  73.5 1.1 slice.152
  74.7 1.3 collective-permute-start.1
  76.4 6.1 %collective-permute-done.1 = bf16[1,1,256,320]{2,3,1,0:T(8,128)(2,1)S(1)} collective-permute-done((bf16[1,1,256,320]{2,3,1,0:T(8,128)(2,1)S(1)}, bf16[1,1,256,320]{2,3,1,0:T(8,128)(2,1)S(1)}, u32[]{:S(2)}, u32[]{:S(2)}) %collective-permute-start.1) | collective-permute-done | bytes 163872 | tf_op jit(solution)/shard_map/ppermute | solution.py:12
  82.5 2.8 fusion.54
  85.4 2.2 collective-permute-start
  87.6 2.6 collective-permute-done
  90.3 0.5 pad.58
  90.8 6.4 %slice.104 = bf16[1,2,128,320]{2,3,1,0:T(8,128)(2,1)} slice(bf16[1,5,257,320]{2,3,1,0:T(8,128)(2,1)S(1)} %pad.58), slice={[0:1:1], [0:4:2], [0:256:2], [0:320:1]} | slice | bytes 327680 | tf_op jit(solution)/shard_map/slice | solution.py:79
  97.2 6.4 %slice.105 = bf16[1,2,128,320]{2,3,1,0:T(8,128)(2,1)} slice(bf16[1,5,257,320]{2,3,1,0:T(8,128)(2,1)S(1)} %pad.58), slice={[0:1:1], [0:4:2], [1:257:2], [0:320:1]} | slice | bytes 327680 | tf_op jit(solution)/shard_map/slice | solution.py:79
  103.6 6.4 %slice.106 = bf16[1,2,128,320]{2,3,1,0:T(8,128)(2,1)} slice(bf16[1,5,257,320]{2,3,1,0:T(8,128)(2,1)S(1)} %pad.58), slice={[0:1:1], [0:4:2], [2:257:2], [0:320:1]} | slice | bytes 327680 | tf_op jit(solution)/shard_map/slice | solution.py:79
  110.1 6.4 %slice.107 = bf16[1,2,128,320]{2,3,1,0:T(8,128)(2,1)} slice(bf16[1,5,257,320]{2,3,1,0:T(8,128)(2,1)S(1)} %pad.58), slice={[0:1:1], [1:5:2], [0:256:2], [0:320:1]} | slice | bytes 327680 | tf_op jit(solution)/shard_map/slice | solution.py:79
  116.4 6.4 %slice.108 = bf16[1,2,128,320]{2,3,1,0:T(8,128)(2,1)} slice(bf16[1,5,257,320]{2,3,1,0:T(8,128)(2,1)S(1)} %pad.58), slice={[0:1:1], [1:5:2], [1:257:2], [0:320:1]} | slice | bytes 327680 | tf_op jit(solution)/shard_map/slice | solution.py:79
  122.8 6.4 %slice.109 = bf16[1,2,128,320]{2,3,1,0:T(8,128)(2,1)} slice(bf16[1,5,257,320]{2,3,1,0:T(8,128)(2,1)S(1)} %pad.58), slice={[0:1:1], [1:5:2], [2:257:2], [0:320:1]} | slice | bytes 327680 | tf_op jit(solution)/shard_map/slice | solution.py:79
  129.3 6.4 %slice.110 = bf16[1,2,128,320]{2,3,1,0:T(8,128)(2,1)} slice(bf16[1,5,257,320]{2,3,1,0:T(8,128)(2,1)S(1)} %pad.58), slice={[0:1:1], [2:5:2], [0:256:2], [0:320:1]} | slice | bytes 327680 | tf_op jit(solution)/shard_map/slice | solution.py:79
  135.7 6.4 %slice.111 = bf16[1,2,128,320]{2,3,1,0:T(8,128)(2,1)} slice(bf16[1,5,257,320]{2,3,1,0:T(8,128)(2,1)S(1)} %pad.58), slice={[0:1:1], [2:5:2], [1:257:2], [0:320:1]} | slice | bytes 327680 | tf_op jit(solution)/shard_map/slice | solution.py:79
  142.1 6.5 %slice.112 = bf16[1,2,128,320]{2,3,1,0:T(8,128)(2,1)} slice(bf16[1,5,257,320]{2,3,1,0:T(8,128)(2,1)S(1)} %pad.58), slice={[0:1:1], [2:5:2], [2:257:2], [0:320:1]} | slice | bytes 327680 | tf_op jit(solution)/shard_map/slice | solution.py:79
  148.6 1.2 convolution_bitcast_fusion.9
  149.8 1.2 convolution_bitcast_fusion.8
  151.1 1.1 convolution_bitcast_fusion.7
  152.1 1.0 convolution_bitcast_fusion.6
  153.2 1.0 convolution_bitcast_fusion.5
  154.2 1.1 convolution_bitcast_fusion.4
  155.3 1.1 convolution_bitcast_fusion.3
  156.4 1.1 convolution_bitcast_fusion.2
  157.4 1.1 convolution_bitcast_fusion.1
  158.5 4.8 %concatenate.14 = f32[2880,320]{0,1:T(8,128)} concatenate(f32[320,320]{0,1:T(8,128)S(1)} %convolution_bitcast_fusion.9, f32[320,320]{0,1:T(8,128)S(1)} %convolution_bitcast_fusion.8, f32[320,320]{0,1:T(8,128)} %convolution_bitcast_fusion.7, f32[320,320]{0,1:T(8,128)} %convolution_bitcast_fusion.6, f32[320,320]{0,1:T(8,128)} %convolution_bitcast_fusion.5, ...), dimensions={0} | concatenate | bytes 7372800 | tf_op jit(solution)/shard_map/concatenate | solution.py:85
  163.3 4.1 %broadcast_multiply_fusion = f32[2880,320]{0,1:T(8,128)} fusion(f32[2880,320]{0,1:T(8,128)} %concatenate.14), kind=kLoop, calls=%fused_computation.6 | loop fusion | flops 921600 | bytes 7372800 | tf_op jit(solution)/shard_map/mul | solution.py:85
  167.4 5.4 %copy.48 = f32[2880,320]{1,0:T(8,128)} copy(f32[2880,320]{0,1:T(8,128)} %broadcast_multiply_fusion) | data formatting | bytes 7372800
  172.9 11.8 %all-reduce.14 = (f32[1,320]{1,0:T(1,128)S(1)}, f32[1,320]{1,0:T(1,128)S(1)}) all-reduce(f32[1,320]{1,0:T(1,128)S(1)} %reduce_sum.93, f32[1,320]{1,0:T(1,128)S(1)} %reduce_sum.96), channel_id=1, replica_groups=mesh['groups'=2,'fsdp'=4,'rep'=4] {'fsdp'}, use_global_device_ids=true, to_apply=%region_7.8 | all-reduce | flops 640 | bytes 5120 | tf_op jit(solution)/shard_map/psum | solution.py:90
  185.6 6.1 %psum.47 = bf16[2,320]{1,0:T(2,128)(2,1)S(1)} all-reduce(bf16[2,320]{1,0:T(2,128)(2,1)S(1)} %fusion.49), channel_id=1, replica_groups=mesh['groups'=2,'fsdp'=4,'rep'=4] {'rep'}, use_global_device_ids=true, to_apply=%region_14.15 | all-reduce | flops 640 | bytes 2560 | tf_op jit(solution)/shard_map/psum | solution.py:104
  191.7 0.6 convert_element_type.55
  192.3 1.3 fusion.19
  193.6 0.7 copy.56
  194.3 0.3 pad.59.clone
  194.6 0.4 reshape.178
  195.1 1.5 copy-done.2
  196.7 1.1 fusion.22
  197.9 56.9 %reduce-scatter.4.cloned.1.call-done = f32[720,320]{1,0:T(8,128)} async-done(((f32[2880,320]{1,0:T(8,128)}), f32[720,320]{1,0:T(8,128)}) %reduce-scatter.4.cloned.1.call-update) | async-done | bytes 921616
  254.8 2.2 copy.49
  257.2 0.9 copy.46
  258.1 33.3 %all-reduce.18.cloned.1.call-done = bf16[720,320]{0,1:T(8,128)(2,1)} async-done(((bf16[720,320]{0,1:T(8,128)(2,1)}), bf16[720,320]{0,1:T(8,128)(2,1)}) %all-reduce.18.cloned.1.call-update) | async-done | bytes 460816 | tf_op jit(solution)/shard_map/psum | solution.py:103
  291.4 2.0 convert_element_type.53
  (68 shorter events, 3.1 us)
Async XLA Ops:
  7.2 51.8 %copy-start = (bf16[1,2,128,320]{2,3,1,0:T(8,128)(2,1)S(1)}, bf16[1,2,128,320]{2,3,1,0:T(8,128)(2,1)}, u32[]{:S(2)}) copy-start(bf16[1,2,128,320]{2,3,1,0:T(8,128)(2,1)} %param.7) | copy-start | bytes 491524
  7.2 48.7 %all-gather.3.cloned.1.call-start = ((), (), s32[]{:S(2)}) async-start(), calls=%async_computation.2 | async-start | bytes 2457600 | tf_op jit(solution)/shard_map/all_gather | solution.py:39
  7.9 246.9 %reduce-scatter.4.cloned.1.call-start = ((), (), s32[]{:S(2)}) async-start(), calls=%async_computation.3 | async-start | bytes 5529600
  58.9 1.4 copy-start.1
  62.7 1.5 copy-start.7
  65.2 1.0 copy-start.5
  65.2 1.1 copy-start.6
  67.6 1.4 copy-start.3
  69.7 6.6 %copy-start.15 = (f32[2,320]{1,0:T(2,128)S(1)}, f32[2,320]{1,0:T(2,128)}, u32[]{:S(2)}) copy-start(f32[2,320]{1,0:T(2,128)} %param.5) | copy-start | bytes 7684
  74.7 7.8 %collective-permute-start.1 = (bf16[1,1,256,320]{2,3,1,0:T(8,128)(2,1)S(1)}, bf16[1,1,256,320]{2,3,1,0:T(8,128)(2,1)S(1)}, u32[]{:S(2)}, u32[]{:S(2)}) collective-permute-start(bf16[1,1,256,320]{2,3,1,0:T(8,128)(2,1)S(1)} %slice.152), channel_id=1, source_target_pairs={{4,0},{8,4},{12,8},{5,1},{9,5},{13,9},{6,2},{10,6},{14,10},{7,3},{... | collective-permute-start | bytes 491528 | tf_op jit(solution)/shard_map/ppermute | solution.py:12
  85.4 4.8 %collective-permute-start = (bf16[1,1,256,320]{2,3,1,0:T(8,128)(2,1)S(1)}, bf16[1,1,256,320]{2,3,1,0:T(8,128)(2,1)S(1)}, u32[]{:S(2)}, u32[]{:S(2)}) collective-permute-start(bf16[1,1,256,320]{2,3,1,0:T(8,128)(2,1)S(1)} %slice.115), channel_id=1, source_target_pairs={{0,4},{4,8},{8,12},{1,5},{5,9},{9,13},{2,6},{6,10},{10,14},{3,7},{... | collective-permute-start | bytes 491528 | tf_op jit(solution)/shard_map/ppermute | solution.py:12
  148.6 2.5 copy-start.14
  148.6 3.5 %copy-start.13 = (bf16[1,2,128,320]{2,3,1,0:T(8,128)(2,1)S(1)}, bf16[1,2,128,320]{2,3,1,0:T(8,128)(2,1)}, u32[]{:S(2)}) copy-start(bf16[1,2,128,320]{2,3,1,0:T(8,128)(2,1)} %slice.107) | copy-start | bytes 491524
  149.8 3.4 %copy-start.12 = (bf16[1,2,128,320]{2,3,1,0:T(8,128)(2,1)S(1)}, bf16[1,2,128,320]{2,3,1,0:T(8,128)(2,1)}, u32[]{:S(2)}) copy-start(bf16[1,2,128,320]{2,3,1,0:T(8,128)(2,1)} %slice.108) | copy-start | bytes 491524
  151.1 3.2 %copy-start.11 = (bf16[1,2,128,320]{2,3,1,0:T(8,128)(2,1)S(1)}, bf16[1,2,128,320]{2,3,1,0:T(8,128)(2,1)}, u32[]{:S(2)}) copy-start(bf16[1,2,128,320]{2,3,1,0:T(8,128)(2,1)} %slice.109) | copy-start | bytes 491524
  152.1 3.2 %copy-start.10 = (bf16[1,2,128,320]{2,3,1,0:T(8,128)(2,1)S(1)}, bf16[1,2,128,320]{2,3,1,0:T(8,128)(2,1)}, u32[]{:S(2)}) copy-start(bf16[1,2,128,320]{2,3,1,0:T(8,128)(2,1)} %slice.110) | copy-start | bytes 491524
  153.2 3.2 %copy-start.9 = (bf16[1,2,128,320]{2,3,1,0:T(8,128)(2,1)S(1)}, bf16[1,2,128,320]{2,3,1,0:T(8,128)(2,1)}, u32[]{:S(2)}) copy-start(bf16[1,2,128,320]{2,3,1,0:T(8,128)(2,1)} %slice.111) | copy-start | bytes 491524
  154.2 3.2 %copy-start.8 = (bf16[1,2,128,320]{2,3,1,0:T(8,128)(2,1)S(1)}, bf16[1,2,128,320]{2,3,1,0:T(8,128)(2,1)}, u32[]{:S(2)}) copy-start(bf16[1,2,128,320]{2,3,1,0:T(8,128)(2,1)} %slice.112) | copy-start | bytes 491524
  172.8 19.4 %copy-start.4 = (bf16[1,4,256,320]{2,3,1,0:T(8,128)(2,1)S(1)}, bf16[1,4,256,320]{2,3,1,0:T(8,128)(2,1)}, u32[]{:S(2)}) copy-start(bf16[1,4,256,320]{2,3,1,0:T(8,128)(2,1)} %param.4) | copy-start | bytes 1966084
  172.9 118.5 %all-reduce.18.cloned.1.call-start = ((), (), s32[]{:S(2)}) async-start(), calls=%async_computation.1 | async-start | bytes 983040 | tf_op jit(solution)/shard_map/psum | solution.py:103
  194.9 1.7 copy-start.2
  195.0 1.7 copy-start.16
Sparse Core Ops, SparseCore 0:
  9.6 46.2 all-gather.2
  173.0 81.7 reduce-scatter.3
  257.9 33.4 all-reduce.17
where the time goes:
time: 301 us; the launch traced here: 300 us
  waiting for transfers between devices  132 us (44%)
  local copies, waits for them, and re-layouts  91.5 us (30%)
  blocking collectives  31.4 us (10%)
  other arithmetic  15.2 us (5%)
  between operations  14.2 us (5%)
  matrix products  11.8 us (4%)
  starting transfers between devices  3.59 us (1%)
    slice x9, local copies, waits for them, and re-layouts, shards(): window = padded_cols[:, row_tap:row_tap + rows:2, col_tap:col_tap + width:2]  57.8 us
    unnamed x4, waiting for transfers between devices  57.6 us
    psum x1, waiting for transfers between devices, shards(): lax.psum(owned.astype(jnp.bfloat16), 'rep').astype(jnp.float32)  33.3 us
    all_gather x1, waiting for transfers between devices, shards(): full_weight = lax.all_gather(conv_weight, 'fsdp', axis=0, tiled=True)  32.5 us
    psum x1, blocking collectives, shards(): sum_one, sum_two = lax.psum((part_one, part_two), 'fsdp')  13.6 us
    unnamed x38, local copies, waits for them, and re-layouts  12.8 us
    psum x1, blocking collectives, shards(): u_sum, v_sum = lax.psum((u_part, v_part), 'fsdp')  11.8 us
    dot_general x9, matrix products, shards(): jnp.einsum('bijc,bijo->co', window, cotangent, preferred_element_type=jnp...  9.83 us
  transfers between devices with their start and end apart: 5, of which 5 were waited for; matrix products, arithmetic and copies ran while one was open for 3% of the time, Pallas kernels for 0%

commit v1 on v0

--- a/solution.py
+++ b/solution.py
@@ -1,9 +1,14 @@
+import functools
+
 import jax
 import jax.numpy as jnp
 from jax import lax
+from jax.experimental import pallas as pl
+from jax.experimental.pallas import tpu as pltpu
 from jax.sharding import PartitionSpec as P
 
 GROUPS = 32
+MESH = pl.DeviceIdType.MESH
 
 
 def passed_along(shard, axis, by):
@@ -106,6 +111,449 @@
     return (output_maps, input_grad, weight_grad, gain_grad)
 
 
+ROW_SLOT = (0, 3, 1, 4, 2)
+TAP_OFF = (0, 3, 1)
+
+
+def dot(lhs, rhs, contract=((1,), (0,)), precision=None):
+    return lax.dot_general(
+        lhs, rhs, (contract, ((), ())), precision=precision, preferred_element_type=jnp.float32
+    )
+
+
+def fused(
+    nz,
+    x_ref,
+    g_ref,
+    w_ref,
+    ct_ref,
+    out_ref,
+    dx_ref,
+    wg_ref,
+    gg_ref,
+    xh,
+    cth,
+    norm,
+    dsilu,
+    zgrad,
+    acts,
+    cts,
+    css,
+    wfull,
+    stat,
+    stat_in,
+    part,
+    core_in,
+    half,
+    x_in,
+    quarter,
+    z_in,
+    final,
+    rep_in,
+    uv,
+    uv_in,
+    uvt,
+    uvt_in,
+    halo_sem,
+    stat_sem,
+    w_sem,
+    tail_sem,
+    core_sem,
+    x_sem,
+    z_sem,
+    rep_sem,
+    uv_sem,
+    uvt_sem,
+    loc_sem,
+):
+    f32, bf16 = jnp.float32, jnp.bfloat16
+    rows, width, chans = x_ref.shape[1:]
+    cols = width // 2
+    block = w_ref.shape[0]
+    quart = quarter.shape[1]
+    step = (block - quart) // 3
+    count = rows * nz * width * (chans // GROUPS)
+    scale = 1.0 / jnp.sqrt(f32(4 * nz * ct_ref.shape[1] * cols))
+    z = lax.axis_index("fsdp")
+    rep = lax.axis_index("rep")
+    xi, ci = rep // 2, rep % 2
+    mine = 2 * ci + xi
+    peers_z = [lax.rem(z + d, nz) for d in range(1, nz)]
+    reps = [(2 * xi + 1 - ci), (2 * (1 - xi) + ci), (2 * (1 - xi) + 1 - ci)]
+    core_peer, x_peer = reps[0], reps[1]
+
+    def aligned(value):
+        return pl.multiple_of(value, 16)
+
+    def remote(src, dst, sem, device):
+        return pltpu.make_async_remote_copy(
+            src_ref=src,
+            dst_ref=dst,
+            send_sem=sem.at[0],
+            recv_sem=sem.at[1],
+            device_id=device,
+            device_id_type=MESH,
+        )
+
+    barrier = pltpu.get_barrier_semaphore()
+    for peer in peers_z:
+        pl.semaphore_signal(barrier, inc=1, device_id={"fsdp": peer}, device_id_type=MESH)
+    for peer in reps:
+        pl.semaphore_signal(barrier, inc=1, device_id={"rep": peer}, device_id_type=MESH)
+
+    own_w = pltpu.make_async_copy(w_ref, wfull.at[pl.ds(aligned(z * block), block)], loc_sem.at[0])
+    own_w.start()
+
+    big_i = lax.broadcasted_iota(jnp.int32, (width, width), 0)
+    big_j = lax.broadcasted_iota(jnp.int32, (width, width), 1)
+    split = jnp.where(
+        jnp.where(big_i < cols, 2 * big_i, 2 * (big_i - cols) + 1) == big_j, 1.0, 0.0
+    ).astype(bf16)
+    merge = jnp.where(
+        jnp.where(big_j < cols, 2 * big_j, 2 * (big_j - cols) + 1) == big_i, 1.0, 0.0
+    ).astype(bf16)
+    inv = 1.0 / (chans // GROUPS)
+    grp_i = jnp.floor((lax.broadcasted_iota(jnp.int32, (chans, chans), 0).astype(f32) + 0.5) * inv)
+    grp_j = jnp.floor((lax.broadcasted_iota(jnp.int32, (chans, chans), 1).astype(f32) + 0.5) * inv)
+    same = jnp.where(grp_i == grp_j, 1.0, 0.0)
+
+    sum_one = jnp.zeros((1, chans), f32)
+    sum_two = jnp.zeros((1, chans), f32)
+    for r in range(rows):
+        x_val = dot(split, x_ref[0, r])
+        norm[r + 1] = x_val
+        sum_one = sum_one + jnp.sum(x_val, axis=0, keepdims=True)
+        sum_two = sum_two + jnp.sum(x_val * x_val, axis=0, keepdims=True)
+    stat[...] = jnp.zeros(stat.shape, f32)
+    stat[0:1] = sum_one
+    stat[1:2] = sum_two
+
+    pl.semaphore_wait(barrier, nz - 1 + 3)
+
+    stat_cp = [
+        remote(stat, stat_in.at[d], stat_sem.at[d], {"fsdp": peers_z[d]}) for d in range(nz - 1)
+    ]
+    for cp in stat_cp:
+        cp.start()
+
+    halo_x = remote(x_ref.at[0, rows - 1], xh, halo_sem.at[0], {"fsdp": lax.rem(z + 1, nz)})
+    halo_c = remote(ct_ref.at[0, 0], cth, halo_sem.at[1], {"fsdp": lax.rem(z + nz - 1, nz)})
+
+    @pl.when(z < nz - 1)
+    def _():
+        halo_x.start()
+
+    @pl.when(z > 0)
+    def _():
+        halo_c.start()
+
+    my_off = step * mine
+    piece = aligned(z * block + my_off)
+    w_cp, tail_cp = [], []
+    for d in range(nz - 1):
+        w_cp.append(
+            remote(
+                w_ref.at[pl.ds(aligned(my_off), step)],
+                wfull.at[pl.ds(piece, step)],
+                w_sem.at[0, d],
+                {"fsdp": peers_z[d]},
+            )
+        )
+        tail = block - 4 * step
+        tail_cp.append(
+            remote(
+                w_ref.at[pl.ds(4 * step, tail)],
+                wfull.at[pl.ds(aligned(z * block + 4 * step), tail)],
+                tail_sem.at[d],
+                {"fsdp": peers_z[d]},
+            )
+        )
+    for d in range(nz - 1):
+        w_cp[d].start()
+        tail_cp[d].start()
+
+    row_id = lax.broadcasted_iota(jnp.int32, (cols, chans), 0)
+
+    @pl.when(z == nz - 1)
+    def _():
+        cth[...] = jnp.zeros(cth.shape, bf16)
+
+    @pl.when(z == 0)
+    def _():
+        xh[...] = jnp.zeros(xh.shape, bf16)
+
+    @pl.when(z < nz - 1)
+    def _():
+        halo_c.wait_recv()
+
+    for i in range(3):
+        value = ct_ref[0, i] if i < 2 else cth[...]
+        cts[i * cols : (i + 1) * cols] = value
+        moved = pltpu.roll(value.astype(f32), cols - 1, axis=0)
+        css[i * cols : (i + 1) * cols] = jnp.where(row_id == cols - 1, 0.0, moved).astype(bf16)
+
+    for cp in stat_cp:
+        cp.wait_recv()
+    total = stat[...]
+    for d in range(nz - 1):
+        total = total + stat_in[d]
+    total = dot(total, same, precision=lax.Precision.HIGHEST)
+    mean = total[0:1] / count
+    rstd = 1.0 / jnp.sqrt(total[1:2] / count - mean * mean + 1e-05)
+    gain = g_ref[0:1]
+    shift = g_ref[1:2]
+
+    for r in (1, 2, 3, 4, 0):
+        if r == 0:
+
+            @pl.when(z > 0)
+            def _():
+                halo_x.wait_recv()
+
+            norm[0] = dot(split, xh[...])
+        slot = ROW_SLOT[r]
+        here = pl.ds(slot * cols, cols)
+        for odd in range(2):
+            part_rows = pl.ds(odd * cols, cols)
+            normed = (norm[r, part_rows] - mean) * rstd
+            z_val = gain * normed + shift
+            sig = 0.5 * jnp.tanh(0.5 * z_val) + 0.5
+            act = z_val * sig
+            if r == 0:
+                act = act * jnp.where(z > 0, 1.0, 0.0)
+            else:
+                norm[r, part_rows] = normed
+                dsilu[r - 1, part_rows] = sig * (1.0 + z_val * (1.0 - sig))
+            acts[1 + odd, here] = act.astype(bf16)
+            if odd == 1:
+                moved = pltpu.roll(act, 1, axis=0)
+                acts[0, here] = jnp.where(row_id == 0, 0.0, moved).astype(bf16)
+
+    grad_rows = cts[0 : 2 * cols]
+    for tap in range(9):
+        lhs = acts[tap % 3, pl.ds(TAP_OFF[tap // 3] * cols, 2 * cols)]
+        part[tap * chans : (tap + 1) * chans] = dot(lhs, grad_rows, ((0,), (0,))).astype(bf16)
+
+    half_rows = half.shape[1]
+    core_cp = []
+    for q in range(nz):
+        core_cp.append(
+            remote(
+                part.at[pl.ds(aligned(q * block + 2 * step * (1 - ci)), half_rows)],
+                core_in.at[q],
+                core_sem.at[q],
+                {"rep": core_peer},
+            )
+        )
+        core_cp[q].start()
+
+    fwd_x, fwd_c, fwd_d = [], [], []
+    x_off = step * (2 * ci + 1 - xi)
+    for d in range(nz - 1):
+        w_cp[d].wait_recv()
+        src_z = lax.rem(z + nz - 1 - d, nz)
+        spot = wfull.at[pl.ds(aligned(src_z * block + my_off), step)]
+        fwd_x.append(remote(spot, spot, w_sem.at[1, d], {"rep": x_peer}))
+        fwd_c.append(remote(spot, spot, w_sem.at[2, d], {"rep": core_peer}))
+        fwd_x[d].start()
+        fwd_c[d].start()
+
+    x_cp = []
+    for q in range(nz):
+        core_cp[q].wait_recv()
+        mine_rows = part[pl.ds(aligned(q * block + 2 * step * ci), half_rows)]
+        half[q] = (mine_rows.astype(f32) + core_in[q].astype(f32)).astype(bf16)
+        x_cp.append(
+            remote(
+                half.at[q, pl.ds(aligned(step * (1 - xi)), quart)],
+                x_in.at[q],
+                x_sem.at[q],
+                {"rep": x_peer},
+            )
+        )
+        x_cp[q].start()
+
+    for d in range(nz - 1):
+        fwd_x[d].wait_recv()
+        src_z = lax.rem(z + nz - 1 - d, nz)
+        spot = wfull.at[pl.ds(aligned(src_z * block + x_off), step)]
+        fwd_d.append(remote(spot, spot, w_sem.at[3, d], {"rep": core_peer}))
+        fwd_d[d].start()
+    own_w.wait()
+    for d in range(nz - 1):
+        tail_cp[d].wait_recv()
+        fwd_c[d].wait_recv()
+        fwd_d[d].wait_recv()
+
+    result = jnp.zeros((2 * cols, wfull.shape[1]), f32)
+    for tap in range(9):
+        lhs = acts[tap % 3, pl.ds(TAP_OFF[tap // 3] * cols, 2 * cols)]
+        result = result + dot(lhs, wfull[tap * chans : (tap + 1) * chans])
+    out_ref[0, 0] = result[:cols].astype(bf16)
+    out_ref[0, 1] = result[cols:].astype(bf16)
+
+    u_sum = jnp.zeros((1, chans), f32)
+    v_sum = jnp.zeros((1, chans), f32)
+
+    def back(source, first, tap):
+        lhs = source[first * cols : (first + 2) * cols]
+        return dot(lhs, wfull[tap * chans : (tap + 1) * chans], ((1,), (1,)))
+
+    for odd_row in range(2):
+        for odd in range(2):
+            if odd_row == 0 and odd == 0:
+                grad = back(cts, 0, 4)
+            elif odd_row == 0:
+                grad = back(cts, 0, 5) + back(css, 0, 3)
+            elif odd == 0:
+                grad = back(cts, 0, 7) + back(cts, 1, 1)
+            else:
+                grad = back(cts, 0, 8) + back(css, 0, 6) + back(cts, 1, 2) + back(css, 1, 0)
+            for i in range(2):
+                r = 2 * i + odd_row
+                part_rows = pl.ds(odd * cols, cols)
+                value = grad[i * cols : (i + 1) * cols] * dsilu[r, part_rows]
+                zgrad[r, part_rows] = value
+                u_sum = u_sum + jnp.sum(value * norm[r + 1, part_rows], axis=0, keepdims=True)
+                v_sum = v_sum + jnp.sum(value, axis=0, keepdims=True)
+    uv[...] = jnp.zeros(uv.shape, f32)
+    uv[0:1] = u_sum
+    uv[1:2] = v_sum
+    uv_cp = [remote(uv, uv_in.at[d], uv_sem.at[d], {"fsdp": peers_z[d]}) for d in range(nz - 1)]
+    for cp in uv_cp:
+        cp.start()
+
+    for q in range(nz):
+        x_cp[q].wait_recv()
+        mine_rows = half[q, pl.ds(aligned(step * xi), quart)]
+        quarter[q] = (mine_rows.astype(f32) + x_in[q].astype(f32)).astype(bf16)
+    z_cp = []
+    for d in range(nz - 1):
+        z_cp.append(
+            remote(quarter.at[peers_z[d]], z_in.at[d], z_sem.at[d], {"fsdp": peers_z[d]})
+        )
+        z_cp[d].start()
+
+    for cp in uv_cp:
+        cp.wait_recv()
+    total = uv[...]
+    for d in range(nz - 1):
+        total = total + uv_in[d]
+    uvt[...] = total
+    uvt_cp = [remote(uvt, uvt_in.at[m], uvt_sem.at[m], {"rep": reps[m]}) for m in range(3)]
+    for cp in uvt_cp:
+        cp.start()
+    grp = dot(gain * total, same, precision=lax.Precision.HIGHEST)
+    su_val = grp[0:1] / count
+    sv_val = grp[1:2] / count
+    for r in range(rows):
+        value = rstd * (gain * zgrad[r] - sv_val - norm[r + 1] * su_val)
+        dx_ref[0, r] = dot(merge, value.astype(bf16)).astype(bf16)
+
+    value = quarter[z].astype(f32)
+    for d in range(nz - 1):
+        z_cp[d].wait_recv()
+        value = value + z_in[d].astype(f32)
+    final[...] = (value * scale).astype(bf16)
+    rep_cp = [remote(final, rep_in.at[m], rep_sem.at[m], {"rep": reps[m]}) for m in range(3)]
+    for cp in rep_cp:
+        cp.start()
+
+    def place(ref, k):
+        wg_ref[pl.ds(pl.multiple_of(step * k, 16), step)] = ref[0:step].astype(f32)
+
+        @pl.when(k == 3)
+        def _():
+            wg_ref[4 * step : block] = ref[step:quart].astype(f32)
+
+    place(final, mine)
+    for cp in uvt_cp:
+        cp.wait_recv()
+    gg_ref[...] = (uvt[0:2] + uvt_in[0, 0:2] + uvt_in[1, 0:2] + uvt_in[2, 0:2]) * scale
+    owners = [2 * (1 - ci) + xi, 2 * ci + 1 - xi, 2 * (1 - ci) + 1 - xi]
+    for m in range(3):
+        rep_cp[m].wait_recv()
+        place(rep_in.at[m], owners[m])
+
+    @pl.when(z < nz - 1)
+    def _():
+        halo_x.wait_send()
+
+    @pl.when(z > 0)
+    def _():
+        halo_c.wait_send()
+
+    for group in (
+        stat_cp, w_cp, tail_cp, core_cp, fwd_x, fwd_c, fwd_d, x_cp, uv_cp, z_cp, uvt_cp, rep_cp
+    ):
+        for cp in group:
+            cp.wait_send()
+
+
+def fused_shards(images, gains, conv_weight, cotangent):
+    batch, rows, width, chans = images.shape
+    outs_ch = conv_weight.shape[1]
+    nz = lax.axis_size("fsdp")
+    block = conv_weight.shape[0]
+    cols = width // 2
+    tiles = block // 16
+    step = 16 * (tiles // 4)
+    quart = block - 3 * step
+    f32, bf16 = jnp.float32, jnp.bfloat16
+    vmem = pltpu.VMEM
+    dma = pltpu.SemaphoreType.DMA
+    return pl.pallas_call(
+        functools.partial(fused, nz),
+        out_shape=(
+            jax.ShapeDtypeStruct((batch, rows // 2, cols, outs_ch), bf16),
+            jax.ShapeDtypeStruct(images.shape, bf16),
+            jax.ShapeDtypeStruct((block, outs_ch), f32),
+            jax.ShapeDtypeStruct(gains.shape, f32),
+        ),
+        in_specs=[pl.BlockSpec(memory_space=vmem)] * 4,
+        out_specs=[pl.BlockSpec(memory_space=vmem)] * 4,
+        scratch_shapes=[
+            vmem((width, chans), bf16),
+            vmem((cols, outs_ch), bf16),
+            vmem((rows + 1, width, chans), f32),
+            vmem((rows, width, chans), f32),
+            vmem((rows, width, chans), f32),
+            vmem((3, 5 * cols, chans), bf16),
+            vmem((3 * cols, outs_ch), bf16),
+            vmem((3 * cols, outs_ch), bf16),
+            vmem((nz * block, outs_ch), bf16),
+            vmem((8, chans), f32),
+            vmem((nz - 1, 8, chans), f32),
+            vmem((nz * block, outs_ch), bf16),
+            vmem((nz, step + quart, outs_ch), bf16),
+            vmem((nz, step + quart, outs_ch), bf16),
+            vmem((nz, quart, outs_ch), bf16),
+            vmem((nz, quart, outs_ch), bf16),
+            vmem((nz - 1, quart, outs_ch), bf16),
+            vmem((quart, outs_ch), bf16),
+            vmem((3, quart, outs_ch), bf16),
+            vmem((8, chans), f32),
+            vmem((nz - 1, 8, chans), f32),
+            vmem((8, chans), f32),
+            vmem((3, 8, chans), f32),
+            dma((2, 2)),
+            dma((nz - 1, 2)),
+            dma((4, nz - 1, 2)),
+            dma((nz - 1, 2)),
+            dma((nz, 2)),
+            dma((nz, 2)),
+            dma((nz - 1, 2)),
+            dma((3, 2)),
+            dma((nz - 1, 2)),
+            dma((3, 2)),
+            dma((1,)),
+        ],
+        compiler_params=pltpu.CompilerParams(
+            collective_id=0, has_side_effects=True, vmem_limit_bytes=48 * 1024 * 1024
+        ),
+    )(images, gains, conv_weight, cotangent)
+
+
 def solution(mesh):
     in_specs = (
         P(("groups", "rep"), "fsdp", None, None),
@@ -119,4 +567,6 @@
         P(("groups", "fsdp"), None),
         P("groups", None),
     )
-    return jax.shard_map(shards, mesh=mesh, in_specs=in_specs, out_specs=out_specs, check_vma=False)
+    small = mesh.shape["rep"] == 4 and mesh.shape["fsdp"] <= 4
+    body = fused_shards if small else shards
+    return jax.shard_map(body, mesh=mesh, in_specs=in_specs, out_specs=out_specs, check_vma=False)

time: 301 us -> 66.2 us (0.22)
  the two profiles are of different devices: /device:TPU:0 before, /device:TPU:17 now
where the time goes in v1:
time: 66.2 us; the launch traced here: 66 us
  Pallas kernels  57 us (86%)
  local copies, waits for them, and re-layouts  8.23 us (12%)
  between operations  0.7 us (1%)
    pallas_call x1, Pallas kernels, fused_shards(): pl.pallas_call(functools.partial(fused, nz), out_shape=(jax.ShapeDtypeStr...  57 us
    pallas_call x3, local copies, waits for them, and re-layouts, fused_shards(): pl.pallas_call(functools.partial(fused, nz), out_shape=(jax.ShapeDtypeStr...  4.15 us
    unnamed x10, local copies, waits for them, and re-layouts  4.08 us

profile of v1, /device:TPU:17, one launch (start us, length us, event | category | flops | bytes accessed | tf_op | source)
XLA Modules:
  0.0 66.0 jit_solution(15531246623037687773)
XLA Ops:
  0.6 0.0 copy-start.2
  0.6 1.1 %copy.10.ct_ref = bf16[1,2,128,320]{3,2,1,0:T(8,128)(2,1)S(1)} copy(bf16[1,2,128,320]{2,3,1,0:T(8,128)(2,1)} %param.7) | data formatting | bytes 327680 | tf_op args[3]
  1.8 0.0 copy-start.1
  1.8 1.3 %copy.9.w_ref = bf16[720,320]{1,0:T(8,128)(2,1)S(1)} copy(bf16[720,320]{0,1:T(8,128)(2,1)} %param.6) | data formatting | bytes 921600 | tf_op args[2]
  3.1 0.0 copy-done.2
  3.1 0.4 copy.8.x_ref
  3.5 0.0 copy-done.1
  3.5 57.0 %shard_map.75 = (bf16[1,2,128,320]{3,2,1,0:T(8,128)(2,1)S(1)}, bf16[1,4,256,320]{3,2,1,0:T(8,128)(2,1)S(1)}, f32[720,320]{1,0:T(8,128)S(1)}, f32[2,320]{1,0:T(2,128)S(1)}) custom-call(bf16[1,4,256,320]{3,2,1,0:T(8,128)(2,1)S(1)} %copy.8.x_ref, f32[2,320]{1,0:T(2,128)S(1)} %copy-done.1, bf16[720,320]{1,0:T(8,128)(2,1)S(1)} %copy.9.w_ref, ...), custom_call_target="tpu_custom_call" | custom-call | tf_op jit(solution)/shard_map/pallas_call | solution.py:505
  60.6 0.0 copy-start
  60.6 0.7 %copy-done = bf16[1,2,128,320]{3,2,1,0:T(8,128)(2,1)} copy-done((bf16[1,2,128,320]{3,2,1,0:T(8,128)(2,1)}, bf16[1,2,128,320]{3,2,1,0:T(8,128)(2,1)S(1)}, u32[]{:S(2)}) %copy-start) | copy-done | bytes 163864
  61.2 1.7 %copy.11 = bf16[1,2,128,320]{2,3,1,0:T(8,128)(2,1)} copy(bf16[1,2,128,320]{3,2,1,0:T(8,128)(2,1)} %copy-done) | data formatting | bytes 327680 | tf_op jit(solution)/shard_map/pallas_call | solution.py:505
  63.0 1.1 %copy.12 = bf16[1,4,256,320]{2,3,1,0:T(8,128)(2,1)} copy(bf16[1,4,256,320]{3,2,1,0:T(8,128)(2,1)S(1)} %get-tuple-element.5) | data formatting | bytes 1310720 | tf_op jit(solution)/shard_map/pallas_call | solution.py:505
  64.1 1.3 %copy.13 = f32[720,320]{0,1:T(8,128)} copy(f32[720,320]{1,0:T(8,128)S(1)} %get-tuple-element.6) | data formatting | bytes 1843200 | tf_op jit(solution)/shard_map/pallas_call | solution.py:505
  65.4 0.6 copy.15
Async XLA Ops:
  0.6 2.5 %copy-start.2 = (bf16[1,4,256,320]{2,3,1,0:T(8,128)(2,1)S(1)}, bf16[1,4,256,320]{2,3,1,0:T(8,128)(2,1)}, u32[]{:S(2)}) copy-start(bf16[1,4,256,320]{2,3,1,0:T(8,128)(2,1)} %param.4) | copy-start | bytes 1966084
  1.8 1.7 %copy-start.1 = (f32[2,320]{1,0:T(2,128)S(1)}, f32[2,320]{1,0:T(2,128)}, u32[]{:S(2)}) copy-start(f32[2,320]{1,0:T(2,128)} %g_ref.1) | copy-start | bytes 7684
  60.6 0.7 %copy-start = (bf16[1,2,128,320]{3,2,1,0:T(8,128)(2,1)}, bf16[1,2,128,320]{3,2,1,0:T(8,128)(2,1)S(1)}, u32[]{:S(2)}) copy-start(bf16[1,2,128,320]{3,2,1,0:T(8,128)(2,1)S(1)} %get-tuple-element.4) | copy-start | bytes 491524

commit v2 on v1

v2 whole, which is shorter than its diff:
```python
import functools

import jax
import jax.numpy as jnp
from jax import lax
from jax.experimental import pallas as pl
from jax.experimental.pallas import tpu as pltpu
from jax.sharding import PartitionSpec as P

GROUPS = 32
MESH = pl.DeviceIdType.MESH


def passed_along(shard, axis, by):
    size = lax.axis_size(axis)
    pairs = [(i, i + by) for i in range(size) if 0 <= i + by < size]
    return lax.ppermute(shard, axis, pairs)


def spread_taps(first, middle, last, axis):
    length = first.shape[axis]
    widths_end = [(0, 0)] * first.ndim
    widths_end[axis] = (0, 1)
    widths_start = [(0, 0)] * first.ndim
    widths_start[axis] = (1, 0)
    even = jnp.pad(first, widths_end) + jnp.pad(last, widths_start)
    odd = jnp.pad(middle, widths_end)
    merged = jnp.stack([even, odd], axis=axis + 1)
    shape = list(even.shape)
    shape[axis] = 2 * (length + 1)
    merged = merged.reshape(shape)
    return lax.slice_in_dim(merged, 0, 2 * length + 1, axis=axis)


def shards(images, gains, conv_weight, cotangent):
    batch, rows, width, chans = images.shape
    outs_ch = conv_weight.shape[1]
    n_fsdp = lax.axis_size("fsdp")
    per_group = chans // GROUPS
    x_val = images.astype(jnp.float32)
    grouped = x_val.reshape(batch, rows, width, GROUPS, per_group)
    part_one = jnp.sum(grouped, axis=(1, 2, 4))
    part_two = jnp.sum(grouped * grouped, axis=(1, 2, 4))
    full_weight = lax.all_gather(conv_weight, "fsdp", axis=0, tiled=True)
    sum_one, sum_two = lax.psum((part_one, part_two), "fsdp")
    count = rows * n_fsdp * width * per_group
    mean = sum_one / count
    rstd = 1.0 / jnp.sqrt(sum_two / count - mean * mean + 1e-05)
    normed_g = (grouped - mean[:, None, None, :, None]) * rstd[:, None, None, :, None]
    normed = normed_g.reshape(x_val.shape)
    z_val = gains[0] * normed + gains[1]
    act = (z_val * jax.nn.sigmoid(z_val)).astype(jnp.bfloat16)
    above = passed_along(act[:, rows - 1 : rows], "fsdp", 1)
    padded = jnp.concatenate([above, act], axis=1)
    kernel = full_weight.reshape(3, 3, chans, outs_ch)
    result = lax.conv_general_dilated(
        padded,
        kernel,
        (2, 2),
        ((0, 0), (1, 0)),
        dimension_numbers=("NHWC", "HWIO", "NHWC"),
        preferred_element_type=jnp.float32,
    )
    output_maps = result.astype(jnp.bfloat16)
    patch_grad = jnp.einsum(
        "bijo,ko->bijk", cotangent, full_weight, preferred_element_type=jnp.float32
    )
    half_rows, half_cols = (cotangent.shape[1], cotangent.shape[2])
    taps = patch_grad.reshape(batch, half_rows, half_cols, 3, 3, chans)
    by_row = [
        spread_taps(
            taps[:, :, :, row_tap, 0], taps[:, :, :, row_tap, 1], taps[:, :, :, row_tap, 2], 2
        )
        for row_tap in range(3)
    ]
    grid = spread_taps(by_row[0], by_row[1], by_row[2], 1)[:, :, 1:]
    from_below = passed_along(grid[:, 0:1].astype(jnp.bfloat16), "fsdp", -1).astype(jnp.float32)
    filler = jnp.zeros((batch, rows - 1, width, chans), jnp.float32)
    act_grad = grid[:, 1:] + jnp.concatenate([filler, from_below], axis=1)
    padded_cols = jnp.pad(padded, ((0, 0), (0, 0), (1, 0), (0, 0)))
    blocks = []
    for row_tap in range(3):
        for col_tap in range(3):
            window = padded_cols[:, row_tap : row_tap + rows : 2, col_tap : col_tap + width : 2]
            blocks.append(
                jnp.einsum("bijc,bijo->co", window, cotangent, preferred_element_type=jnp.float32)
            )
    total_pixels = batch * lax.axis_size("rep") * half_rows * n_fsdp * half_cols
    scale = 1.0 / jnp.sqrt(jnp.float32(total_pixels))
    weight_term = jnp.concatenate(blocks, axis=0) * scale
    sig = jax.nn.sigmoid(z_val)
    z_grad = act_grad * sig * (1.0 + z_val * (1.0 - sig))
    u_part = jnp.sum(z_grad * normed, axis=(1, 2))
    v_part = jnp.sum(z_grad, axis=(1, 2))
    u_sum, v_sum = lax.psum((u_part, v_part), "fsdp")
    gain_term = jnp.stack([jnp.sum(u_sum, axis=0), jnp.sum(v_sum, axis=0)]) * scale
    su_val = jnp.sum((gains[0] * u_sum).reshape(batch, GROUPS, per_group), axis=-1)
    sv_val = jnp.sum((gains[0] * v_sum).reshape(batch, GROUPS, per_group), axis=-1)
    scaled = (gains[0] * z_grad).reshape(grouped.shape)
    dx_val = rstd[:, None, None, :, None] * (
        scaled
        - sv_val[:, None, None, :, None] / count
        - normed_g * su_val[:, None, None, :, None] / count
    )
    input_grad = dx_val.reshape(x_val.shape).astype(jnp.bfloat16)
    owned = lax.psum_scatter(weight_term, "fsdp", scatter_dimension=0, tiled=True)
    weight_grad, gain_grad = (
        lax.psum(owned.astype(jnp.bfloat16), "rep").astype(jnp.float32),
        lax.psum(gain_term.astype(jnp.bfloat16), "rep").astype(jnp.float32),
    )
    return (output_maps, input_grad, weight_grad, gain_grad)


HIGHEST = lax.Precision.HIGHEST


def dot(lhs, rhs, contract=((1,), (0,)), precision=None):
    return lax.dot_general(
        lhs, rhs, (contract, ((), ())), precision=precision, preferred_element_type=jnp.float32
    )


def fused(
    nz,
    x_ref,
    g_ref,
    w_ref,
    ct_ref,
    out_ref,
    dx_ref,
    wg_ref,
    gg_ref,
    xh,
    cth,
    norm,
    dsilu,
    zgrad,
    patches,
    cts,
    taps,
    edge,
    wfull,
    stat,
    stat_in,
    part,
    core_in,
    half,
    x_in,
    quarter,
    z_in,
    final,
    rep_in,
    uv,
    uv_in,
    uvt,
    uvt_in,
    halo_sem,
    stat_sem,
    w_sem,
    core_sem,
    x_sem,
    z_sem,
    rep_sem,
    uv_sem,
    uvt_sem,
    loc_sem,
):
    f32, bf16 = jnp.float32, jnp.bfloat16
    rows, chans, width = x_ref.shape[1:]
    cols = width // 2
    outs_ch, block = w_ref.shape
    q_rows = outs_ch // 4
    h_rows = outs_ch // 2
    count = rows * nz * width * (chans // GROUPS)
    scale = 1.0 / jnp.sqrt(f32(4 * nz * ct_ref.shape[1] * cols))
    z = lax.axis_index("fsdp")
    rep = lax.axis_index("rep")
    yi = lax.axis_index("groups")
    xi, ci = rep // 2, rep % 2
    mine = 2 * ci + xi
    peers_z = [lax.rem(z + d, nz) for d in range(1, nz)]
    reps = [(2 * xi + 1 - ci), (2 * (1 - xi) + ci), (2 * (1 - xi) + 1 - ci)]
    core_peer, x_peer = reps[0], reps[1]
    order = [2, 1] + list(range(3, nz)) + [0]

    def aligned(value):
        return pl.multiple_of(value, 16)

    def remote(src, dst, sem, device):
        return pltpu.make_async_remote_copy(
            src_ref=src,
            dst_ref=dst,
            send_sem=sem.at[0],
            recv_sem=sem.at[1],
            device_id=device,
            device_id_type=MESH,
        )

    barrier = pltpu.get_barrier_semaphore()
    for peer in peers_z:
        pl.semaphore_signal(barrier, inc=1, device_id={"fsdp": peer}, device_id_type=MESH)
    for peer in reps:
        pl.semaphore_signal(barrier, inc=1, device_id={"rep": peer}, device_id_type=MESH)
    pl.semaphore_signal(barrier, inc=1, device_id={"groups": 1 - yi}, device_id_type=MESH)

    own_w = pltpu.make_async_copy(w_ref, wfull.at[z], loc_sem.at[0])
    own_w.start()

    big_i = lax.broadcasted_iota(jnp.int32, (width, width), 0)
    big_j = lax.broadcasted_iota(jnp.int32, (width, width), 1)
    split = jnp.where(
        jnp.where(big_j < cols, 2 * big_j, 2 * (big_j - cols) + 1) == big_i, 1.0, 0.0
    ).astype(bf16)
    merge = jnp.where(
        jnp.where(big_i < cols, 2 * big_i, 2 * (big_i - cols) + 1) == big_j, 1.0, 0.0
    ).astype(bf16)
    inv = 1.0 / (chans // GROUPS)
    ch_i = lax.broadcasted_iota(jnp.int32, (chans, chans), 0)
    ch_j = lax.broadcasted_iota(jnp.int32, (chans, chans), 1)
    grp_i = jnp.floor((ch_i.astype(f32) + 0.5) * inv)
    grp_j = jnp.floor((ch_j.astype(f32) + 0.5) * inv)
    same = jnp.where(grp_i == grp_j, 1.0, 0.0)
    eye = jnp.where(ch_i == ch_j, 1.0, 0.0)
    ones = jnp.ones((8, cols), f32)

    def row_sums(value):
        return dot(ones, value, ((1,), (1,)), HIGHEST)

    sum_one = jnp.zeros((chans, cols), f32)
    sum_two = jnp.zeros((chans, cols), f32)
    for r in range(rows):
        x_val = dot(x_ref[0, r], split)
        norm[r + 1] = x_val
        even, odd = x_val[:, :cols], x_val[:, cols:]
        sum_one = sum_one + (even + odd)
        sum_two = sum_two + (even * even + odd * odd)
    stat[0:8] = row_sums(sum_one)
    stat[8:16] = row_sums(sum_two)

    pl.semaphore_wait(barrier, nz - 1 + 3 + 1)

    stat_cp = [
        remote(stat, stat_in.at[d], stat_sem.at[d], {"fsdp": peers_z[d]}) for d in range(nz - 1)
    ]
    for cp in stat_cp:
        cp.start()

    halo_x = remote(x_ref.at[0, rows - 1], xh, halo_sem.at[0], {"fsdp": lax.rem(z + 1, nz)})
    halo_c = remote(ct_ref.at[0, 0], cth, halo_sem.at[1], {"fsdp": lax.rem(z + nz - 1, nz)})

    @pl.when(z < nz - 1)
    def _():
        halo_x.start()

    @pl.when(z > 0)
    def _():
        halo_c.start()

    w_off = aligned(q_rows * (2 * ci + yi))
    w_cp = []
    for d in range(nz - 1):
        w_cp.append(
            remote(
                w_ref.at[pl.ds(w_off, q_rows)],
                wfull.at[z, pl.ds(w_off, q_rows)],
                w_sem.at[0, d],
                {"fsdp": peers_z[d]},
            )
        )
        w_cp[d].start()

    lane = lax.broadcasted_iota(jnp.int32, (chans, cols), 1)

    @pl.when(z == nz - 1)
    def _():
        cth[...] = jnp.zeros(cth.shape, bf16)

    @pl.when(z == 0)
    def _():
        xh[...] = jnp.zeros(xh.shape, bf16)

    for i in range(2):
        cts[:, i * cols : (i + 1) * cols] = ct_ref[0, i]
    gains = dot(eye, g_ref[...], ((1,), (1,)), HIGHEST)
    gain = jnp.broadcast_to(gains[:, 0:1], (chans, cols))
    shift = jnp.broadcast_to(gains[:, 1:2], (chans, cols))

    for cp in stat_cp:
        cp.wait_recv()
    total = stat[...]
    for d in range(nz - 1):
        total = total + stat_in[d]
    total = dot(same, total, ((1,), (1,)), HIGHEST)
    mean = total[:, 0:1] / count
    rstd = 1.0 / jnp.sqrt(total[:, 8:9] / count - mean * mean + 1e-05)
    mean = jnp.broadcast_to(mean, (chans, cols))
    rstd = jnp.broadcast_to(rstd, (chans, cols))

    def put(row_tap, col_tap, i, value):
        tap = 3 * row_tap + col_tap
        patches[tap * chans : (tap + 1) * chans, i * cols : (i + 1) * cols] = value

    users = [[(t, i) for i in range(2) for t in range(3) if 2 * i + t == r] for r in range(5)]
    for r in (1, 2, 3, 4, 0):
        if r == 0:

            @pl.when(z > 0)
            def _():
                halo_x.wait_recv()

            norm[0] = dot(xh[...], split)
        for odd in range(2):
            here = pl.ds(odd * cols, cols)
            normed = (norm[r, :, here] - mean) * rstd
            z_val = gain * normed + shift
            sig = 0.5 * jnp.tanh(0.5 * z_val) + 0.5
            act = z_val * sig
            if r == 0:
                act = act * jnp.where(z > 0, 1.0, 0.0)
            else:
                norm[r, :, here] = normed
                dsilu[r - 1, :, here] = sig * (1.0 + z_val * (1.0 - sig))
            rounded = act.astype(bf16)
            for t, i in users[r]:
                put(t, 1 + odd, i, rounded)
            if odd == 1:
                moved = pltpu.roll(act, 1, axis=1)
                moved = jnp.where(lane == 0, 0.0, moved).astype(bf16)
                for t, i in users[r]:
                    put(t, 0, i, moved)

    fwd_y, fwd_c, fwd_d = [], [], []

    def forward_first(d):
        w_cp[d].wait_recv()
        src_z = lax.rem(z + nz - 1 - d, nz)
        spot = wfull.at[src_z, pl.ds(w_off, q_rows)]
        fwd_y.append(remote(spot, spot, w_sem.at[1, d], {"groups": 1 - yi}))
        fwd_c.append(remote(spot, spot, w_sem.at[2, d], {"rep": core_peer}))
        fwd_y[d].start()
        fwd_c[d].start()

    def forward_second(d):
        fwd_y[d].wait_recv()
        src_z = lax.rem(z + nz - 1 - d, nz)
        spot = wfull.at[src_z, pl.ds(aligned(q_rows * (2 * ci + 1 - yi)), q_rows)]
        fwd_d.append(remote(spot, spot, w_sem.at[3, d], {"rep": core_peer}))
        fwd_d[d].start()

    core_cp, x_cp, z_cp = [], [], []

    def core_step(n):
        d = order[n]
        q = lax.rem(z + d, nz)
        core_cp[n].wait_recv()
        mine_rows = part[q, pl.ds(aligned(h_rows * ci), h_rows)]
        half[n] = (mine_rows.astype(f32) + core_in[n].astype(f32)).astype(bf16)
        x_cp.append(
            remote(
                half.at[n, pl.ds(aligned(q_rows * (1 - xi)), q_rows)],
                x_in.at[n],
                x_sem.at[n],
                {"rep": x_peer},
            )
        )
        x_cp[n].start()

    def x_step(n):
        d = order[n]
        x_cp[n].wait_recv()
        mine_rows = half[n, pl.ds(aligned(q_rows * xi), q_rows)]
        value = mine_rows.astype(f32) + x_in[n].astype(f32)
        quarter[n] = value.astype(bf16)
        if d > 0:
            z_cp.append(
                remote(quarter.at[n], z_in.at[d - 1], z_sem.at[d - 1], {"fsdp": peers_z[d - 1]})
            )
            z_cp[n].start()

    for n, d in enumerate(order):
        q = lax.rem(z + d, nz)
        rhs = patches[pl.ds(aligned(q * block), block)]
        part[q] = dot(cts[:, : 2 * cols], rhs, ((1,), (1,))).astype(bf16)
        core_cp.append(
            remote(
                part.at[q, pl.ds(aligned(h_rows * (1 - ci)), h_rows)],
                core_in.at[n],
                core_sem.at[n],
                {"rep": core_peer},
            )
        )
        core_cp[n].start()
        if n > 0:
            core_step(n - 1)
    core_step(nz - 1)
    for d in range(nz - 1):
        forward_first(d)
    x_step(0)
    for d in range(nz - 1):
        forward_second(d)
    x_step(1)
    own_w.wait()
    for d in range(nz - 1):
        fwd_c[d].wait_recv()
        fwd_d[d].wait_recv()

    grads = cts[:, : 2 * cols]
    result = jnp.zeros((outs_ch, 2 * cols), f32)
    for q in range(nz):
        result = result + dot(wfull[q], patches[q * block : (q + 1) * block])
    out_ref[0, 0] = result[:, :cols].astype(bf16)
    out_ref[0, 1] = result[:, cols:].astype(bf16)
    for n in range(2, nz):
        x_step(n)

    for q in range(nz):
        taps[q * block : (q + 1) * block] = dot(wfull[q], grads, ((0,), (0,)))

    @pl.when(z < nz - 1)
    def _():
        halo_c.wait_recv()

    below = cth[...]
    done = 0
    q = 0
    while done < 3 * chans:
        take = min(block, 3 * chans - done)
        edge[done : done + take] = dot(wfull[q, :, :take], below, ((0,), (0,)))
        done += take
        q += 1

    def tap_at(row_tap, col_tap, i):
        tap = 3 * row_tap + col_tap
        here = slice(tap * chans, (tap + 1) * chans)
        if i == 2:
            return edge[here]
        return taps[here, i * cols : (i + 1) * cols]

    u_sum = jnp.zeros((chans, cols), f32)
    v_sum = jnp.zeros((chans, cols), f32)
    for r in range(rows):
        pairs = [(t, i) for i in range(3) for t in range(3) if 2 * i + t == r + 1]
        for odd in range(2):
            here = pl.ds(odd * cols, cols)
            grad = sum(tap_at(t, 1 + odd, i) for t, i in pairs)
            if odd == 1:
                left = sum(tap_at(t, 0, i) for t, i in pairs)
                moved = pltpu.roll(left, cols - 1, axis=1)
                grad = grad + jnp.where(lane == cols - 1, 0.0, moved)
            value = grad * dsilu[r, :, here]
            zgrad[r, :, here] = value
            u_sum = u_sum + value * norm[r + 1, :, here]
            v_sum = v_sum + value
    uv[0:8] = row_sums(u_sum)
    uv[8:16] = row_sums(v_sum)
    uv_cp = [remote(uv, uv_in.at[d], uv_sem.at[d], {"fsdp": peers_z[d]}) for d in range(nz - 1)]
    for cp in uv_cp:
        cp.start()

    value = quarter[nz - 1].astype(f32)
    for n in range(nz - 1):
        z_cp[n].wait_recv()
    for d in range(nz - 1):
        value = value + z_in[d].astype(f32)
    final[...] = (value * scale).astype(bf16)
    rep_cp = [remote(final, rep_in.at[m], rep_sem.at[m], {"rep": reps[m]}) for m in range(2)]
    for cp in rep_cp:
        cp.start()

    for cp in uv_cp:
        cp.wait_recv()
    total = uv[...]
    for d in range(nz - 1):
        total = total + uv_in[d]
    uvt[...] = total
    uvt_cp = [remote(uvt, uvt_in.at[m], uvt_sem.at[m], {"rep": reps[m]}) for m in range(3)]
    for cp in uvt_cp:
        cp.start()
    grp = dot(same, g_ref[0:1] * total, ((1,), (1,)), HIGHEST)
    su_val = jnp.broadcast_to(grp[:, 0:1] / count, (chans, cols))
    sv_val = jnp.broadcast_to(grp[:, 8:9] / count, (chans, cols))
    rep_cp[1].wait_recv()
    rep_cp.append(remote(rep_in.at[1], rep_in.at[2], rep_sem.at[2], {"rep": core_peer}))
    rep_cp[2].start()

    for r in range(rows):
        for odd in range(2):
            here = pl.ds(odd * cols, cols)
            value = rstd * (gain * zgrad[r, :, here] - sv_val - norm[r + 1, :, here] * su_val)
            patches[r * chans : (r + 1) * chans, here] = value.astype(bf16)
        dx_ref[0, r] = dot(patches[r * chans : (r + 1) * chans], merge).astype(bf16)

    def place(ref, k):
        wg_ref[pl.ds(aligned(q_rows * k), q_rows)] = ref[...].astype(f32)

    place(final, mine)
    for cp in uvt_cp:
        cp.wait_recv()
    total = uvt[...] + uvt_in[0] + uvt_in[1] + uvt_in[2]
    gg_ref[0:1] = total[0:1] * scale
    gg_ref[1:2] = total[8:9] * scale
    owners = [2 * (1 - ci) + xi, 2 * ci + 1 - xi, 2 * (1 - ci) + 1 - xi]
    for m in range(3):
        if m != 1:
            rep_cp[m].wait_recv()
        place(rep_in.at[m], owners[m])

    @pl.when(z < nz - 1)
    def _():
        halo_x.wait_send()

    @pl.when(z > 0)
    def _():
        halo_c.wait_send()

    for group in (
        stat_cp, w_cp, core_cp, fwd_y, fwd_c, fwd_d, x_cp, uv_cp, z_cp, uvt_cp, rep_cp
    ):
        for cp in group:
            cp.wait_send()


def fused_shards(images, gains, conv_weight, cotangent):
    batch, rows, width, chans = images.shape
    block, outs_ch = conv_weight.shape
    if (batch, rows, cotangent.shape[1]) != (1, 4, 2) or block % 16 or outs_ch % 64:
        return shards(images, gains, conv_weight, cotangent)
    nz = lax.axis_size("fsdp")
    cols = width // 2
    q_rows = outs_ch // 4
    f32, bf16 = jnp.float32, jnp.bfloat16
    vmem = pltpu.VMEM
    dma = pltpu.SemaphoreType.DMA
    output_maps, input_grad, weight_grad, gain_grad = pl.pallas_call(
        functools.partial(fused, nz),
        out_shape=(
            jax.ShapeDtypeStruct((batch, rows // 2, outs_ch, cols), bf16),
            jax.ShapeDtypeStruct((batch, rows, chans, width), bf16),
            jax.ShapeDtypeStruct((outs_ch, block), f32),
            jax.ShapeDtypeStruct(gains.shape, f32),
        ),
        in_specs=[pl.BlockSpec(memory_space=vmem)] * 4,
        out_specs=[pl.BlockSpec(memory_space=vmem)] * 4,
        scratch_shapes=[
            vmem((chans, width), bf16),
            vmem((outs_ch, cols), bf16),
            vmem((rows + 1, chans, width), f32),
            vmem((rows, chans, width), f32),
            vmem((rows, chans, width), f32),
            vmem((nz * block, width), bf16),
            vmem((outs_ch, width), bf16),
            vmem((nz * block, width), f32),
            vmem((3 * chans, cols), f32),
            vmem((nz, outs_ch, block), bf16),
            vmem((16, chans), f32),
            vmem((nz - 1, 16, chans), f32),
            vmem((nz, outs_ch, block), bf16),
            vmem((nz, 2 * q_rows, block), bf16),
            vmem((nz, 2 * q_rows, block), bf16),
            vmem((nz, q_rows, block), bf16),
            vmem((nz, q_rows, block), bf16),
            vmem((nz - 1, q_rows, block), bf16),
            vmem((q_rows, block), bf16),
            vmem((3, q_rows, block), bf16),
            vmem((16, chans), f32),
            vmem((nz - 1, 16, chans), f32),
            vmem((16, chans), f32),
            vmem((3, 16, chans), f32),
            dma((2, 2)),
            dma((nz - 1, 2)),
            dma((4, nz - 1, 2)),
            dma((nz, 2)),
            dma((nz, 2)),
            dma((nz - 1, 2)),
            dma((3, 2)),
            dma((nz - 1, 2)),
            dma((3, 2)),
            dma((1,)),
        ],
        compiler_params=pltpu.CompilerParams(
            collective_id=0, has_side_effects=True, vmem_limit_bytes=48 * 1024 * 1024
        ),
    )(
        jnp.swapaxes(images, 2, 3),
        gains,
        conv_weight.T,
        jnp.swapaxes(cotangent, 2, 3),
    )
    return (
        jnp.swapaxes(output_maps, 2, 3),
        jnp.swapaxes(input_grad, 2, 3),
        weight_grad.T,
        gain_grad,
    )


def solution(mesh):
    in_specs = (
        P(("groups", "rep"), "fsdp", None, None),
        P(),
        P("fsdp", None),
        P(("groups", "rep"), "fsdp", None, None),
    )
    out_specs = (
        P(("groups", "rep"), "fsdp", None, None),
        P(("groups", "rep"), "fsdp", None, None),
        P(("groups", "fsdp"), None),
        P("groups", None),
    )
    small = mesh.shape["groups"] == 2 and mesh.shape["rep"] == 4 and mesh.shape["fsdp"] == 4
    body = fused_shards if small else shards
    return jax.shard_map(body, mesh=mesh, in_specs=in_specs, out_specs=out_specs, check_vma=False)
```

time: 66.2 us -> 51.9 us (0.78)
  the two profiles are of different devices: /device:TPU:17 before, /device:TPU:0 now
where the time goes in v2:
time: 51.9 us; the launch traced here: 51.7 us
  Pallas kernels  44.3 us (85%)
  local copies, waits for them, and re-layouts  6.73 us (13%)
  between operations  0.65 us (1%)
    pallas_call x1, Pallas kernels, fused_shards(): pl.pallas_call(functools.partial(fused, nz), out_shape=(jax.ShapeDtypeStr...  44.3 us
    unnamed x12, local copies, waits for them, and re-layouts  6.73 us

profile of v2, /device:TPU:0, one launch (start us, length us, event | category | flops | bytes accessed | tf_op | source)
XLA Modules:
  0.0 51.7 jit_solution(15926065053434376306)
XLA Ops:
  0.6 0.0 copy-start.3
  0.6 0.7 %copy-done.3 = f32[2,320]{1,0:T(2,128)S(1)} copy-done((f32[2,320]{1,0:T(2,128)S(1)}, f32[2,320]{1,0:T(2,128)}, u32[]{:S(2)}) %copy-start.3) | copy-done | bytes 2584
  1.3 0.0 copy-start
  1.3 1.1 %copy-done = bf16[1,4,256,320]{2,3,1,0:T(8,128)(2,1)S(1)} copy-done((bf16[1,4,256,320]{2,3,1,0:T(8,128)(2,1)S(1)}, bf16[1,4,256,320]{2,3,1,0:T(8,128)(2,1)}, u32[]{:S(2)}) %copy-start) | copy-done | bytes 655384
  2.4 0.0 copy-start.1
  2.4 1.0 %copy-done.1 = bf16[720,320]{0,1:T(8,128)(2,1)S(1)} copy-done((bf16[720,320]{0,1:T(8,128)(2,1)S(1)}, bf16[720,320]{0,1:T(8,128)(2,1)}, u32[]{:S(2)}) %copy-start.1) | copy-done | bytes 460824
  3.4 0.0 copy-start.2
  3.4 0.9 %copy-done.2 = bf16[1,2,128,320]{2,3,1,0:T(8,128)(2,1)S(1)} copy-done((bf16[1,2,128,320]{2,3,1,0:T(8,128)(2,1)S(1)}, bf16[1,2,128,320]{2,3,1,0:T(8,128)(2,1)}, u32[]{:S(2)}) %copy-start.2) | copy-done | bytes 163864
  4.4 44.3 %shard_map.75 = (bf16[1,2,320,128]{3,2,1,0:T(8,128)(2,1)S(1)}, bf16[1,4,320,256]{3,2,1,0:T(8,128)(2,1)S(1)}, f32[320,720]{1,0:T(8,128)S(1)}, f32[2,320]{1,0:T(2,128)S(1)}) custom-call(bf16[1,4,320,256]{3,2,1,0:T(8,128)(2,1)S(1)} %bitcast.8, f32[2,320]{1,0:T(2,128)S(1)} %copy-done.3, bf16[320,720]{1,0:T(8,128)(2,1)S(1)} %bitcast.9, ...), custom_call_target="tpu_custom_call" | custom-call | tf_op jit(solution)/shard_map/pallas_call | solution.py:534
  48.7 0.7 %copy.12 = bf16[1,2,128,320]{2,3,1,0:T(8,128)(2,1)} copy(bf16[1,2,128,320]{2,3,1,0:T(8,128)(2,1)S(1)} %bitcast.11) | data formatting | bytes 327680
  49.3 0.8 %copy.13 = bf16[1,4,256,320]{2,3,1,0:T(8,128)(2,1)} copy(bf16[1,4,256,320]{2,3,1,0:T(8,128)(2,1)S(1)} %bitcast.7) | data formatting | bytes 1310720
  50.2 0.9 %copy.14 = f32[720,320]{0,1:T(8,128)} copy(f32[720,320]{0,1:T(8,128)S(1)} %bitcast.6) | data formatting | bytes 1843200
  51.1 0.6 %copy.15 = f32[2,320]{1,0:T(2,128)} copy(f32[2,320]{1,0:T(2,128)S(1)} %get-tuple-element.19) | data formatting | bytes 5120
Async XLA Ops:
  0.6 0.7 %copy-start.3 = (f32[2,320]{1,0:T(2,128)S(1)}, f32[2,320]{1,0:T(2,128)}, u32[]{:S(2)}) copy-start(f32[2,320]{1,0:T(2,128)} %g_ref.1) | copy-start | bytes 7684
  1.3 1.1 %copy-start = (bf16[1,4,256,320]{2,3,1,0:T(8,128)(2,1)S(1)}, bf16[1,4,256,320]{2,3,1,0:T(8,128)(2,1)}, u32[]{:S(2)}) copy-start(bf16[1,4,256,320]{2,3,1,0:T(8,128)(2,1)} %param.4) | copy-start | bytes 1966084
  2.4 1.0 %copy-start.1 = (bf16[720,320]{0,1:T(8,128)(2,1)S(1)}, bf16[720,320]{0,1:T(8,128)(2,1)}, u32[]{:S(2)}) copy-start(bf16[720,320]{0,1:T(8,128)(2,1)} %param.6) | copy-start | bytes 1382404
  3.4 0.9 %copy-start.2 = (bf16[1,2,128,320]{2,3,1,0:T(8,128)(2,1)S(1)}, bf16[1,2,128,320]{2,3,1,0:T(8,128)(2,1)}, u32[]{:S(2)}) copy-start(bf16[1,2,128,320]{2,3,1,0:T(8,128)(2,1)} %param.7) | copy-start | bytes 491524

commit v3 on v2

--- a/solution.py
+++ b/solution.py
@@ -267,6 +267,8 @@
                 {"fsdp": peers_z[d]},
             )
         )
+
+    for d in reversed(range(nz - 1)):
         w_cp[d].start()
 
     lane = lax.broadcasted_iota(jnp.int32, (chans, cols), 1)
@@ -398,7 +400,8 @@
     x_step(0)
     for d in range(nz - 1):
         forward_second(d)
-    x_step(1)
+    for n in range(1, nz):
+        x_step(n)
     own_w.wait()
     for d in range(nz - 1):
         fwd_c[d].wait_recv()
@@ -410,9 +413,6 @@
         result = result + dot(wfull[q], patches[q * block : (q + 1) * block])
     out_ref[0, 0] = result[:, :cols].astype(bf16)
     out_ref[0, 1] = result[:, cols:].astype(bf16)
-    for n in range(2, nz):
-        x_step(n)
-
     for q in range(nz):
         taps[q * block : (q + 1) * block] = dot(wfull[q], grads, ((0,), (0,)))
 

time: 51.9 us -> 50.9 us (0.981)
  Pallas kernels: 44.3 us -> 43.2 us
    pallas_call x1, Pallas kernels: 44.3 us -> 43.2 us  [fused_shards(): pl.pallas_call(functools.partial(fused, nz), out_shape=(jax.ShapeDtypeStr...]
where the time goes in v3:
time: 50.9 us; the launch traced here: 50.6 us
  Pallas kernels  43.2 us (85%)
  local copies, waits for them, and re-layouts  6.73 us (13%)
  between operations  0.65 us (1%)
    pallas_call x1, Pallas kernels, fused_shards(): pl.pallas_call(functools.partial(fused, nz), out_shape=(jax.ShapeDtypeStr...  43.2 us
    unnamed x12, local copies, waits for them, and re-layouts  6.73 us

profile of v3, /device:TPU:0, one launch (start us, length us, event | category | flops | bytes accessed | tf_op | source)
XLA Modules:
  0.0 50.6 jit_solution(4678939238485587924)
XLA Ops:
  0.6 0.0 copy-start.3
  0.6 0.7 %copy-done.3 = f32[2,320]{1,0:T(2,128)S(1)} copy-done((f32[2,320]{1,0:T(2,128)S(1)}, f32[2,320]{1,0:T(2,128)}, u32[]{:S(2)}) %copy-start.3) | copy-done | bytes 2584
  1.3 0.0 copy-start
  1.3 1.1 %copy-done = bf16[1,4,256,320]{2,3,1,0:T(8,128)(2,1)S(1)} copy-done((bf16[1,4,256,320]{2,3,1,0:T(8,128)(2,1)S(1)}, bf16[1,4,256,320]{2,3,1,0:T(8,128)(2,1)}, u32[]{:S(2)}) %copy-start) | copy-done | bytes 655384
  2.4 0.0 copy-start.1
  2.4 1.0 %copy-done.1 = bf16[720,320]{0,1:T(8,128)(2,1)S(1)} copy-done((bf16[720,320]{0,1:T(8,128)(2,1)S(1)}, bf16[720,320]{0,1:T(8,128)(2,1)}, u32[]{:S(2)}) %copy-start.1) | copy-done | bytes 460824
  3.4 0.0 copy-start.2
  3.4 0.9 %copy-done.2 = bf16[1,2,128,320]{2,3,1,0:T(8,128)(2,1)S(1)} copy-done((bf16[1,2,128,320]{2,3,1,0:T(8,128)(2,1)S(1)}, bf16[1,2,128,320]{2,3,1,0:T(8,128)(2,1)}, u32[]{:S(2)}) %copy-start.2) | copy-done | bytes 163864
  4.4 43.2 %shard_map.75 = (bf16[1,2,320,128]{3,2,1,0:T(8,128)(2,1)S(1)}, bf16[1,4,320,256]{3,2,1,0:T(8,128)(2,1)S(1)}, f32[320,720]{1,0:T(8,128)S(1)}, f32[2,320]{1,0:T(2,128)S(1)}) custom-call(bf16[1,4,320,256]{3,2,1,0:T(8,128)(2,1)S(1)} %bitcast.8, f32[2,320]{1,0:T(2,128)S(1)} %copy-done.3, bf16[320,720]{1,0:T(8,128)(2,1)S(1)} %bitcast.9, ...), custom_call_target="tpu_custom_call" | custom-call | tf_op jit(solution)/shard_map/pallas_call | solution.py:534
  47.6 0.7 %copy.12 = bf16[1,2,128,320]{2,3,1,0:T(8,128)(2,1)} copy(bf16[1,2,128,320]{2,3,1,0:T(8,128)(2,1)S(1)} %bitcast.11) | data formatting | bytes 327680
  48.3 0.8 %copy.13 = bf16[1,4,256,320]{2,3,1,0:T(8,128)(2,1)} copy(bf16[1,4,256,320]{2,3,1,0:T(8,128)(2,1)S(1)} %bitcast.7) | data formatting | bytes 1310720
  49.1 0.9 %copy.14 = f32[720,320]{0,1:T(8,128)} copy(f32[720,320]{0,1:T(8,128)S(1)} %bitcast.6) | data formatting | bytes 1843200
  50.0 0.6 %copy.15 = f32[2,320]{1,0:T(2,128)} copy(f32[2,320]{1,0:T(2,128)S(1)} %get-tuple-element.19) | data formatting | bytes 5120
Async XLA Ops:
  0.6 0.7 %copy-start.3 = (f32[2,320]{1,0:T(2,128)S(1)}, f32[2,320]{1,0:T(2,128)}, u32[]{:S(2)}) copy-start(f32[2,320]{1,0:T(2,128)} %g_ref.1) | copy-start | bytes 7684
  1.3 1.1 %copy-start = (bf16[1,4,256,320]{2,3,1,0:T(8,128)(2,1)S(1)}, bf16[1,4,256,320]{2,3,1,0:T(8,128)(2,1)}, u32[]{:S(2)}) copy-start(bf16[1,4,256,320]{2,3,1,0:T(8,128)(2,1)} %param.4) | copy-start | bytes 1966084
  2.4 1.0 %copy-start.1 = (bf16[720,320]{0,1:T(8,128)(2,1)S(1)}, bf16[720,320]{0,1:T(8,128)(2,1)}, u32[]{:S(2)}) copy-start(bf16[720,320]{0,1:T(8,128)(2,1)} %param.6) | copy-start | bytes 1382404
  3.4 0.9 %copy-start.2 = (bf16[1,2,128,320]{2,3,1,0:T(8,128)(2,1)S(1)}, bf16[1,2,128,320]{2,3,1,0:T(8,128)(2,1)}, u32[]{:S(2)}) copy-start(bf16[1,2,128,320]{2,3,1,0:T(8,128)(2,1)} %param.7) | copy-start | bytes 491524

commit v4 on v3

--- a/solution.py
+++ b/solution.py
@@ -252,10 +252,6 @@
     def _():
         halo_x.start()
 
-    @pl.when(z > 0)
-    def _():
-        halo_c.start()
-
     w_off = aligned(q_rows * (2 * ci + yi))
     w_cp = []
     for d in range(nz - 1):
@@ -270,6 +266,10 @@
 
     for d in reversed(range(nz - 1)):
         w_cp[d].start()
+
+    @pl.when(z > 0)
+    def _():
+        halo_c.start()
 
     lane = lax.broadcasted_iota(jnp.int32, (chans, cols), 1)
 

time: 50.9 us -> 50.9 us (level)
  no operation moved by 1% of the time
where the time goes in v4:
time: 50.9 us; the launch traced here: 50.6 us
  Pallas kernels  43.2 us (85%)
  local copies, waits for them, and re-layouts  6.73 us (13%)
  between operations  0.65 us (1%)
    pallas_call x1, Pallas kernels, fused_shards(): pl.pallas_call(functools.partial(fused, nz), out_shape=(jax.ShapeDtypeStr...  43.2 us
    unnamed x12, local copies, waits for them, and re-layouts  6.73 us

profile of v4, /device:TPU:0, one launch (start us, length us, event | category | flops | bytes accessed | tf_op | source)
XLA Modules:
  0.0 50.6 jit_solution(5134920209426908127)
XLA Ops:
  0.6 0.0 copy-start.3
  0.6 0.7 %copy-done.3 = f32[2,320]{1,0:T(2,128)S(1)} copy-done((f32[2,320]{1,0:T(2,128)S(1)}, f32[2,320]{1,0:T(2,128)}, u32[]{:S(2)}) %copy-start.3) | copy-done | bytes 2584
  1.3 0.0 copy-start
  1.3 1.1 %copy-done = bf16[1,4,256,320]{2,3,1,0:T(8,128)(2,1)S(1)} copy-done((bf16[1,4,256,320]{2,3,1,0:T(8,128)(2,1)S(1)}, bf16[1,4,256,320]{2,3,1,0:T(8,128)(2,1)}, u32[]{:S(2)}) %copy-start) | copy-done | bytes 655384
  2.4 0.0 copy-start.1
  2.4 1.0 %copy-done.1 = bf16[720,320]{0,1:T(8,128)(2,1)S(1)} copy-done((bf16[720,320]{0,1:T(8,128)(2,1)S(1)}, bf16[720,320]{0,1:T(8,128)(2,1)}, u32[]{:S(2)}) %copy-start.1) | copy-done | bytes 460824
  3.4 0.0 copy-start.2
  3.4 0.9 %copy-done.2 = bf16[1,2,128,320]{2,3,1,0:T(8,128)(2,1)S(1)} copy-done((bf16[1,2,128,320]{2,3,1,0:T(8,128)(2,1)S(1)}, bf16[1,2,128,320]{2,3,1,0:T(8,128)(2,1)}, u32[]{:S(2)}) %copy-start.2) | copy-done | bytes 163864
  4.4 43.2 %shard_map.75 = (bf16[1,2,320,128]{3,2,1,0:T(8,128)(2,1)S(1)}, bf16[1,4,320,256]{3,2,1,0:T(8,128)(2,1)S(1)}, f32[320,720]{1,0:T(8,128)S(1)}, f32[2,320]{1,0:T(2,128)S(1)}) custom-call(bf16[1,4,320,256]{3,2,1,0:T(8,128)(2,1)S(1)} %bitcast.8, f32[2,320]{1,0:T(2,128)S(1)} %copy-done.3, bf16[320,720]{1,0:T(8,128)(2,1)S(1)} %bitcast.9, ...), custom_call_target="tpu_custom_call" | custom-call | tf_op jit(solution)/shard_map/pallas_call | solution.py:534
  47.6 0.7 %copy.12 = bf16[1,2,128,320]{2,3,1,0:T(8,128)(2,1)} copy(bf16[1,2,128,320]{2,3,1,0:T(8,128)(2,1)S(1)} %bitcast.11) | data formatting | bytes 327680
  48.3 0.8 %copy.13 = bf16[1,4,256,320]{2,3,1,0:T(8,128)(2,1)} copy(bf16[1,4,256,320]{2,3,1,0:T(8,128)(2,1)S(1)} %bitcast.7) | data formatting | bytes 1310720
  49.1 0.9 %copy.14 = f32[720,320]{0,1:T(8,128)} copy(f32[720,320]{0,1:T(8,128)S(1)} %bitcast.6) | data formatting | bytes 1843200
  50.0 0.6 %copy.15 = f32[2,320]{1,0:T(2,128)} copy(f32[2,320]{1,0:T(2,128)S(1)} %get-tuple-element.19) | data formatting | bytes 5120
Async XLA Ops:
  0.6 0.7 %copy-start.3 = (f32[2,320]{1,0:T(2,128)S(1)}, f32[2,320]{1,0:T(2,128)}, u32[]{:S(2)}) copy-start(f32[2,320]{1,0:T(2,128)} %g_ref.1) | copy-start | bytes 7684
  1.3 1.1 %copy-start = (bf16[1,4,256,320]{2,3,1,0:T(8,128)(2,1)S(1)}, bf16[1,4,256,320]{2,3,1,0:T(8,128)(2,1)}, u32[]{:S(2)}) copy-start(bf16[1,4,256,320]{2,3,1,0:T(8,128)(2,1)} %param.4) | copy-start | bytes 1966084
  2.4 1.0 %copy-start.1 = (bf16[720,320]{0,1:T(8,128)(2,1)S(1)}, bf16[720,320]{0,1:T(8,128)(2,1)}, u32[]{:S(2)}) copy-start(bf16[720,320]{0,1:T(8,128)(2,1)} %param.6) | copy-start | bytes 1382404
  3.4 0.9 %copy-start.2 = (bf16[1,2,128,320]{2,3,1,0:T(8,128)(2,1)S(1)}, bf16[1,2,128,320]{2,3,1,0:T(8,128)(2,1)}, u32[]{:S(2)}) copy-start(bf16[1,2,128,320]{2,3,1,0:T(8,128)(2,1)} %param.7) | copy-start | bytes 491524
